TPU v7x, 32 devices: a whole 2x2x4 slice. The times are simulated.
32 devices in a mesh: grp: 4 (over x, core), uly: 8 (over z, y).
Axes of the slice: x: 2, y: 2, z: 4, core: 2. Of those that a mesh axis runs over, the one named last changes fastest.
Arguments:
- queries: bfloat16 [4096, 8192], P(('grp', 'uly')), may hold values from -6 to 6
- key_state_rows: bfloat16 [4096, 1024], P(('grp', 'uly')), may hold values from -6 to 6
- value_state_rows: bfloat16 [4096, 1024], P(('grp', 'uly')), may hold values from -6 to 6
- vert_blocks: int32 [64, 6], replicated, may hold values from -1 to 31, as said below
- slash_offsets: int32 [64, 3], replicated, may hold values from -1 to 4, as said below
Outputs:
- attended: bfloat16 [4096, 8192], P(('grp', 'uly'))
Inputs may be any that keep to these rules, and one draw needn't show every extreme that they name: `vert_blocks`: row h lists distinct block numbers first and -1 in the slots after them; every row lists one block or more and some row lists 6. `slash_offsets`: row h lists distinct offsets of at least 1 first and -1 in the slots after them; every row lists one offset or more and some row lists 3.
All inputs are finite; a program needn't handle non-finite values.
Results may differ from a plain program's by a relative error of at most 0.005.
Values may be sent and summed in bfloat16 or wider, within the bound.
A program may use at most 128 MiB of HBM per device.

v0:
```python
import jax
import jax.numpy as jnp
import numpy as np
from jax import lax
from jax.sharding import PartitionSpec as P

QUERY_HEADS = 64
KEY_VALUE_HEADS = 8
HEAD_SIZE = 128
BLOCK_TOKENS = 128


neg_large = -1e30


def passed_along(value, axis, steps):
    count = lax.axis_size(axis)
    initial, last = (max(0, -steps), min(count, count - steps))
    return lax.ppermute(value, axis, [(source, source + steps) for source in range(initial, last)])


def add_slot(running, slot_scores, allowed, weigh):
    best, total, accum = running
    slot_scores = jnp.where(allowed, slot_scores, neg_large)
    new_best = jnp.maximum(best, jnp.max(slot_scores, axis=-1))
    factor = jnp.exp(best - new_best)
    weights = jnp.where(allowed, jnp.exp(slot_scores - new_best[..., None]), 0.0)
    total = total * factor + jnp.sum(weights, axis=-1)
    accum = accum * factor[..., None] + weigh(weights.astype(jnp.bfloat16))
    return (new_best, total, accum)


def shards(queries, key_state_rows, value_state_rows, vert_blocks, slash_offsets):
    ulysses_count = lax.axis_size("uly")
    group_id = lax.axis_index("grp")
    uly_id = lax.axis_index("uly")
    per_device = QUERY_HEADS // ulysses_count
    group_width = QUERY_HEADS // KEY_VALUE_HEADS
    token_rows = queries.shape[0]
    ordering = jnp.arange(QUERY_HEADS, dtype=jnp.int32)
    heads_per_slot = np.arange(ulysses_count) * per_device // group_width
    key_outgoing = key_state_rows.reshape(token_rows, KEY_VALUE_HEADS, HEAD_SIZE)[
        :, heads_per_slot
    ].reshape(token_rows, ulysses_count * HEAD_SIZE)
    value_outgoing = value_state_rows.reshape(token_rows, KEY_VALUE_HEADS, HEAD_SIZE)[
        :, heads_per_slot
    ].reshape(token_rows, ulysses_count * HEAD_SIZE)
    q_group, k_group, v_group = (
        lax.all_to_all(queries, "uly", split_axis=1, concat_axis=0, tiled=True),
        lax.all_to_all(key_outgoing, "uly", split_axis=1, concat_axis=0, tiled=True),
        lax.all_to_all(value_outgoing, "uly", split_axis=1, concat_axis=0, tiled=True),
    )
    seg_rows = q_group.shape[0]
    block_count = seg_rows // BLOCK_TOKENS
    reach = block_count // 2
    q_tiles = q_group.reshape(block_count, BLOCK_TOKENS, per_device, HEAD_SIZE)
    key_block_tiles = k_group.reshape(block_count, BLOCK_TOKENS, HEAD_SIZE)
    value_block_tiles = v_group.reshape(block_count, BLOCK_TOKENS, HEAD_SIZE)
    prior_k, prior_v = passed_along(
        (key_block_tiles[block_count - reach :], value_block_tiles[block_count - reach :]), "grp", 1
    )
    k_wide = jnp.concatenate([prior_k, key_block_tiles], axis=0)
    v_wide = jnp.concatenate([prior_v, value_block_tiles], axis=0)
    heads_here = lax.dynamic_slice_in_dim(ordering, uly_id * per_device, per_device)
    vert_list = jnp.take(vert_blocks, heads_here, axis=0)
    offset_list = jnp.take(slash_offsets, heads_here, axis=0)
    local_block = jnp.where(vert_list >= 0, vert_list % block_count, 0)
    owned = (vert_list >= 0) & (vert_list // block_count == group_id)
    pick_k = jnp.where(
        owned[:, :, None, None], key_block_tiles[local_block], jnp.zeros((), jnp.bfloat16)
    )
    pick_v = jnp.where(
        owned[:, :, None, None], value_block_tiles[local_block], jnp.zeros((), jnp.bfloat16)
    )
    summed_k, summed_v = (
        lax.psum(pick_k.astype(jnp.float32).astype(jnp.bfloat16), "grp").astype(jnp.float32),
        lax.psum(pick_v.astype(jnp.float32).astype(jnp.bfloat16), "grp").astype(jnp.float32),
    )
    vert_k = summed_k.astype(jnp.bfloat16)
    vert_v = summed_v.astype(jnp.bfloat16)
    query_blocks = group_id * block_count + jnp.arange(block_count, dtype=jnp.int32)
    score_scale = HEAD_SIZE ** (-0.5)
    causal = (jnp.arange(BLOCK_TOKENS)[:, None] >= jnp.arange(BLOCK_TOKENS)[None, :])[
        None, :, None, :
    ]
    diag_scores = (
        jnp.einsum("nqhd,nkd->nqhk", q_tiles, key_block_tiles, preferred_element_type=jnp.float32)
        * score_scale
    )
    diag_scores = jnp.where(causal, diag_scores, neg_large)
    best = jnp.max(diag_scores, axis=-1)
    diag_weights = jnp.where(causal, jnp.exp(diag_scores - best[..., None]), 0.0)
    total = jnp.sum(diag_weights, axis=-1)
    accum = jnp.einsum(
        "nqhk,nkd->nqhd",
        diag_weights.astype(jnp.bfloat16),
        value_block_tiles,
        preferred_element_type=jnp.float32,
    )
    running = (best, total, accum)

    def slash_slot(slot_index, running):
        offset_now = lax.dynamic_index_in_dim(offset_list, slot_index, axis=1, keepdims=False)
        starts = jnp.where(offset_now >= 1, reach - offset_now, 0)

        def near_slice(begin_at):
            return (
                lax.dynamic_slice_in_dim(k_wide, begin_at, block_count, 0),
                lax.dynamic_slice_in_dim(v_wide, begin_at, block_count, 0),
            )

        k_near, v_near = jax.vmap(near_slice)(starts)
        allowed = (offset_now[None, :] >= 1) & (query_blocks[:, None] - offset_now[None, :] >= 0)
        slot_scores = (
            jnp.einsum("nqhd,hnkd->nqhk", q_tiles, k_near, preferred_element_type=jnp.float32)
            * score_scale
        )

        def weigh_near(prob_low):
            return jnp.einsum(
                "nqhk,hnkd->nqhd", prob_low, v_near, preferred_element_type=jnp.float32
            )

        return add_slot(running, slot_scores, allowed[:, None, :, None], weigh_near)

    slash_turns = jnp.max(jnp.sum((offset_list >= 1).astype(jnp.int32), axis=1))
    running = lax.fori_loop(0, slash_turns, slash_slot, running)

    def vert_slot(slot_index, running):
        block_now = lax.dynamic_index_in_dim(vert_list, slot_index, axis=1, keepdims=False)
        k_far = lax.dynamic_index_in_dim(vert_k, slot_index, axis=1, keepdims=False)
        v_far = lax.dynamic_index_in_dim(vert_v, slot_index, axis=1, keepdims=False)
        hits = (offset_list[None, :, :] >= 1) & (
            query_blocks[:, None, None] - offset_list[None, :, :] == block_now[None, :, None]
        )
        allowed = (
            (block_now[None, :] >= 0)
            & (block_now[None, :] < query_blocks[:, None])
            & jnp.logical_not(jnp.any(hits, axis=2))
        )
        slot_scores = (
            jnp.einsum("nqhd,hkd->nqhk", q_tiles, k_far, preferred_element_type=jnp.float32)
            * score_scale
        )

        def weigh_far(prob_low):
            return jnp.einsum("nqhk,hkd->nqhd", prob_low, v_far, preferred_element_type=jnp.float32)

        return add_slot(running, slot_scores, allowed[:, None, :, None], weigh_far)

    vert_turns = jnp.max(jnp.sum((vert_list >= 0).astype(jnp.int32), axis=1))
    best, total, accum = lax.fori_loop(0, vert_turns, vert_slot, running)
    mixed = (
        (accum / total[..., None]).astype(jnp.bfloat16).reshape(seg_rows, per_device * HEAD_SIZE)
    )
    returned = lax.all_to_all(mixed, "uly", split_axis=0, concat_axis=1, tiled=True)
    return returned


def solution(mesh):
    return jax.shard_map(
        shards,
        mesh=mesh,
        in_specs=(
            P(("grp", "uly"), None),
            P(("grp", "uly"), None),
            P(("grp", "uly"), None),
            P(),
            P(),
        ),
        out_specs=P(("grp", "uly"), None),
        check_vma=False,
    )
```

profile of v0, /device:TPU:0, one launch (start us, length us, event | category | flops | bytes accessed | tf_op | source)
XLA Modules:
  0.0 279.1 jit_solution(6959106423648515036)
XLA Ops:
  9.3 7.3 %all-to-all-start = ((bf16[128,8,128]{2,0,1:T(8,128)(2,1)}), bf16[128,8,128]{2,0,1:T(8,128)(2,1)S(1)}, u32[]{:S(2)}, u32[]{:S(2)}) async-start(bf16[128,8,128]{2,0,1:T(8,128)(2,1)} %bitcast.1), calls=%async_computation | async-start | bytes 524288 | tf_op jit(solution)/shard_map/all_to_all | solution.py:50
  19.2 6.3 %all-to-all-done = bf16[128,8,128]{2,0,1:T(8,128)(2,1)S(1)} async-done(((bf16[128,8,128]{2,0,1:T(8,128)(2,1)}), bf16[128,8,128]{2,0,1:T(8,128)(2,1)S(1)}, u32[]{:S(2)}, u32[]{:S(2)}) %all-to-all-start) | async-done | bytes 262176 | tf_op jit(solution)/shard_map/all_to_all | solution.py:50
  25.5 3.6 %all-to-all-start.2 = ((bf16[128,8,128]{2,0,1:T(8,128)(2,1)}), bf16[128,8,128]{2,0,1:T(8,128)(2,1)S(1)}, u32[]{:S(2)}, u32[]{:S(2)}) async-start(bf16[128,8,128]{2,0,1:T(8,128)(2,1)} %bitcast.10), calls=%async_computation.2 | async-start | bytes 524288 | tf_op jit(solution)/shard_map/all_to_all | solution.py:51
  31.6 6.1 %all-to-all-done.2 = bf16[128,8,128]{2,0,1:T(8,128)(2,1)S(1)} async-done(((bf16[128,8,128]{2,0,1:T(8,128)(2,1)}), bf16[128,8,128]{2,0,1:T(8,128)(2,1)S(1)}, u32[]{:S(2)}, u32[]{:S(2)}) %all-to-all-start.2) | async-done | bytes 262176 | tf_op jit(solution)/shard_map/all_to_all | solution.py:51
  37.7 3.6 %all-to-all-start.1 = ((bf16[128,8,1024]{0,2,1:T(8,128)(2,1)}), bf16[128,8,1024]{0,2,1:T(8,128)(2,1)S(1)}, u32[]{:S(2)}, u32[]{:S(2)}) async-start(bf16[128,8,1024]{0,2,1:T(8,128)(2,1)} %bitcast.136), calls=%async_computation.1 | async-start | bytes 4194304 | tf_op jit(solution)/shard_map/all_to_all | solution.py:49
  50.2 4.8 %collective-permute-start.1 = (bf16[4,128,128]{2,1,0:T(8,128)(2,1)S(1)}, bf16[4,128,128]{2,1,0:T(8,128)(2,1)}, u32[]{:S(2)}, u32[]{:S(2)}) collective-permute-start(bf16[4,128,128]{2,1,0:T(8,128)(2,1)S(1)} %slice.27), channel_id=1, source_target_pairs={{0,8},{8,16},{16,24},{1,9},{9,17},{17,25},{2,10},{10,18},{18,26},{... | collective-permute-start | bytes 393224 | tf_op jit(solution)/shard_map/ppermute | solution.py:19
  60.2 3.8 %broadcast_select_fusion = (bf16[8,6,128,128]{2,3,0,1:T(8,128)(2,1)}, bf16[8,6,128,128]{2,3,0,1:T(8,128)(2,1)}) fusion(bf16[8,6,128,128]{2,3,0,1:T(8,128)(2,1)} %copy.107, pred[8,6]{0,1:T(8,128)(4,1)S(1)} %copy.105, bf16[8,6,128,128]{2,3,0,1:T(8,128)(2,1)} %copy.106), kind=kLoop, calls=%fused_computation.86 | loop fusion | flops 1572864 | bytes 6291504 | tf_op jit(solution)/shard_map/jit(_where)/select_n | solution.py:72
  65.0 24.1 %all-to-all-done.1 = bf16[128,8,1024]{0,2,1:T(8,128)(2,1)S(1)} async-done(((bf16[128,8,1024]{0,2,1:T(8,128)(2,1)}), bf16[128,8,1024]{0,2,1:T(8,128)(2,1)S(1)}, u32[]{:S(2)}, u32[]{:S(2)}) %all-to-all-start.1) | async-done | bytes 2097184 | tf_op jit(solution)/shard_map/all_to_all | solution.py:49
  96.9 49.3 %while.30 = (s32[]{:T(128)}, f32[8,128,8]{1,2,0:T(8,128)S(1)}, f32[8,128,8]{1,2,0:T(8,128)S(1)}, f32[8,128,8,128]{1,3,2,0:T(8,128)}, s32[]{:T(128)}, /*index=5*/...) while((s32[]{:T(128)}, f32[8,128,8]{1,2,0:T(8,128)S(1)}, ...), condition=%wide.region_7.8_spmd.clone, body=%wide.region_4.7_spmd.clone.sunk | while | flops 552616192 | bytes 52953984 | solution.py:127
  98.8 3.2 %bitcast_reduce_fusion.2 = (f32[8,128,8]{1,2,0:T(8,128)S(1)}, f32[8,8,128,128]{3,2,1,0:T(8,128)S(1)}) fusion(pred[8,8]{1,0:T(8,128)(4,1)S(1)} %fusion.87, bf16[8,128,8,128]{3,1,2,0:T(8,128)(2,1)} %get-tuple-element.511, bf16[8,8,128,128]{3,2,1,0:T(8,128)(2,1)S(1)} %gather_fusion), kind=kOutput, calls=%fused_computation.12.clone.1 | convolution fusion | flops 271572992 | bytes 8421440 | tf_op jit(solution)/shard_map/while/body/nqhd,hnkd->nqhk/dot_general | solution.py:115
  106.0 7.3 %bitcast_add_fusion.4 = f32[8,128,8,128]{1,3,2,0:T(8,128)} fusion(f32[8,128,8,128]{1,3,2,0:T(8,128)} %get-tuple-element.494, f32[8,8,128,128]{3,2,1,0:T(8,128)} %copy-done, bf16[8,8,128,128]{3,2,1,0:T(8,128)(2,1)S(1)} %gather_fusion.1, f32[8,128,8]{1,2,0:T(8,128)S(1)} %get-tuple-element.460, f32[8,128,8]{1,2,0:T(8,128)S(1)} %max.10, ...), kind=kOutput, calls=%fused_computation.10.clone.1 | convolution fusion | flops 275775488 | bytes 14745664 | tf_op jit(solution)/shard_map/while/body/nqhk,hnkd->nqhd/dot_general | solution.py:120
  115.1 3.2 %bitcast_reduce_fusion.2 = (f32[8,128,8]{1,2,0:T(8,128)S(1)}, f32[8,8,128,128]{3,2,1,0:T(8,128)S(1)}) fusion(pred[8,8]{1,0:T(8,128)(4,1)S(1)} %fusion.87, bf16[8,128,8,128]{3,1,2,0:T(8,128)(2,1)} %get-tuple-element.511, bf16[8,8,128,128]{3,2,1,0:T(8,128)(2,1)S(1)} %gather_fusion), kind=kOutput, calls=%fused_computation.12.clone.1 | convolution fusion | flops 271572992 | bytes 8421440 | tf_op jit(solution)/shard_map/while/body/nqhd,hnkd->nqhk/dot_general | solution.py:115
  122.4 7.1 %bitcast_add_fusion.4 = f32[8,128,8,128]{1,3,2,0:T(8,128)} fusion(f32[8,128,8,128]{1,3,2,0:T(8,128)} %get-tuple-element.494, f32[8,8,128,128]{3,2,1,0:T(8,128)} %copy-done, bf16[8,8,128,128]{3,2,1,0:T(8,128)(2,1)S(1)} %gather_fusion.1, f32[8,128,8]{1,2,0:T(8,128)S(1)} %get-tuple-element.460, f32[8,128,8]{1,2,0:T(8,128)S(1)} %max.10, ...), kind=kOutput, calls=%fused_computation.10.clone.1 | convolution fusion | flops 275775488 | bytes 14745664 | tf_op jit(solution)/shard_map/while/body/nqhk,hnkd->nqhd/dot_general | solution.py:120
  131.2 3.2 %bitcast_reduce_fusion.2 = (f32[8,128,8]{1,2,0:T(8,128)S(1)}, f32[8,8,128,128]{3,2,1,0:T(8,128)S(1)}) fusion(pred[8,8]{1,0:T(8,128)(4,1)S(1)} %fusion.87, bf16[8,128,8,128]{3,1,2,0:T(8,128)(2,1)} %get-tuple-element.511, bf16[8,8,128,128]{3,2,1,0:T(8,128)(2,1)S(1)} %gather_fusion), kind=kOutput, calls=%fused_computation.12.clone.1 | convolution fusion | flops 271572992 | bytes 8421440 | tf_op jit(solution)/shard_map/while/body/nqhd,hnkd->nqhk/dot_general | solution.py:115
  138.5 7.0 %bitcast_add_fusion.4 = f32[8,128,8,128]{1,3,2,0:T(8,128)} fusion(f32[8,128,8,128]{1,3,2,0:T(8,128)} %get-tuple-element.494, f32[8,8,128,128]{3,2,1,0:T(8,128)} %copy-done, bf16[8,8,128,128]{3,2,1,0:T(8,128)(2,1)S(1)} %gather_fusion.1, f32[8,128,8]{1,2,0:T(8,128)S(1)} %get-tuple-element.460, f32[8,128,8]{1,2,0:T(8,128)S(1)} %max.10, ...), kind=kOutput, calls=%fused_computation.10.clone.1 | convolution fusion | flops 275775488 | bytes 14745664 | tf_op jit(solution)/shard_map/while/body/nqhk,hnkd->nqhd/dot_general | solution.py:120
  149.2 4.6 %copy.110 = f32[8,128,8,128]{1,3,0,2:T(8,128)} copy(f32[8,128,8,128]{1,3,2,0:T(8,128)} %get-tuple-element.250) | data formatting | bytes 8388608
  153.9 60.6 %while.31 = (s32[]{:T(128)}, f32[8,128,8]{1,0,2:T(8,128)S(1)}, f32[8,128,8]{1,0,2:T(8,128)S(1)}, f32[8,128,8,128]{1,3,0,2:T(8,128)}, s32[]{:T(128)}, /*index=5*/...) while((s32[]{:T(128)}, f32[8,128,8]{1,0,2:T(8,128)S(1)}, ...), condition=%wide.region_16.17_spmd.clone, body=%wide.region_12.16_spmd.clone.sunk | while | flops 552616960 | bytes 57672916 | solution.py:152
  158.7 3.2 %bitcast_add_fusion.5 = f32[8,128,8,128]{1,3,0,2:T(8,128)S(1)} fusion(f32[8,128,8,128]{1,3,0,2:T(8,128)S(1)} %copy-done.1, f32[8,128,8,128]{3,1,2,0:T(8,128)S(1)} %get-tuple-element.475, f32[8,128,8]{1,0,2:T(8,128)S(1)} %get-tuple-element.477, f32[8,128,8]{1,0,2:T(8,128)S(1)} %max.11, pred[8,8]{0,1:T(8,128)(4,1)S(1)} %copy.144, ...), kind=kOutput, calls=%fused_computation.41.clone.1 | convolution fusion | flops 275775488 | bytes 12910660 | tf_op jit(solution)/shard_map/while/body/nqhk,hkd->nqhd/dot_general | solution.py:147
  168.7 3.2 %bitcast_add_fusion.5 = f32[8,128,8,128]{1,3,0,2:T(8,128)S(1)} fusion(f32[8,128,8,128]{1,3,0,2:T(8,128)S(1)} %copy-done.1, f32[8,128,8,128]{3,1,2,0:T(8,128)S(1)} %get-tuple-element.475, f32[8,128,8]{1,0,2:T(8,128)S(1)} %get-tuple-element.477, f32[8,128,8]{1,0,2:T(8,128)S(1)} %max.11, pred[8,8]{0,1:T(8,128)(4,1)S(1)} %copy.144, ...), kind=kOutput, calls=%fused_computation.41.clone.1 | convolution fusion | flops 275775488 | bytes 12910660 | tf_op jit(solution)/shard_map/while/body/nqhk,hkd->nqhd/dot_general | solution.py:147
  178.7 3.2 %bitcast_add_fusion.5 = f32[8,128,8,128]{1,3,0,2:T(8,128)S(1)} fusion(f32[8,128,8,128]{1,3,0,2:T(8,128)S(1)} %copy-done.1, f32[8,128,8,128]{3,1,2,0:T(8,128)S(1)} %get-tuple-element.475, f32[8,128,8]{1,0,2:T(8,128)S(1)} %get-tuple-element.477, f32[8,128,8]{1,0,2:T(8,128)S(1)} %max.11, pred[8,8]{0,1:T(8,128)(4,1)S(1)} %copy.144, ...), kind=kOutput, calls=%fused_computation.41.clone.1 | convolution fusion | flops 275775488 | bytes 12910660 | tf_op jit(solution)/shard_map/while/body/nqhk,hkd->nqhd/dot_general | solution.py:147
  188.7 3.2 %bitcast_add_fusion.5 = f32[8,128,8,128]{1,3,0,2:T(8,128)S(1)} fusion(f32[8,128,8,128]{1,3,0,2:T(8,128)S(1)} %copy-done.1, f32[8,128,8,128]{3,1,2,0:T(8,128)S(1)} %get-tuple-element.475, f32[8,128,8]{1,0,2:T(8,128)S(1)} %get-tuple-element.477, f32[8,128,8]{1,0,2:T(8,128)S(1)} %max.11, pred[8,8]{0,1:T(8,128)(4,1)S(1)} %copy.144, ...), kind=kOutput, calls=%fused_computation.41.clone.1 | convolution fusion | flops 275775488 | bytes 12910660 | tf_op jit(solution)/shard_map/while/body/nqhk,hkd->nqhd/dot_general | solution.py:147
  198.7 3.2 %bitcast_add_fusion.5 = f32[8,128,8,128]{1,3,0,2:T(8,128)S(1)} fusion(f32[8,128,8,128]{1,3,0,2:T(8,128)S(1)} %copy-done.1, f32[8,128,8,128]{3,1,2,0:T(8,128)S(1)} %get-tuple-element.475, f32[8,128,8]{1,0,2:T(8,128)S(1)} %get-tuple-element.477, f32[8,128,8]{1,0,2:T(8,128)S(1)} %max.11, pred[8,8]{0,1:T(8,128)(4,1)S(1)} %copy.144, ...), kind=kOutput, calls=%fused_computation.41.clone.1 | convolution fusion | flops 275775488 | bytes 12910660 | tf_op jit(solution)/shard_map/while/body/nqhk,hkd->nqhd/dot_general | solution.py:147
  208.6 3.2 %bitcast_add_fusion.5 = f32[8,128,8,128]{1,3,0,2:T(8,128)S(1)} fusion(f32[8,128,8,128]{1,3,0,2:T(8,128)S(1)} %copy-done.1, f32[8,128,8,128]{3,1,2,0:T(8,128)S(1)} %get-tuple-element.475, f32[8,128,8]{1,0,2:T(8,128)S(1)} %get-tuple-element.477, f32[8,128,8]{1,0,2:T(8,128)S(1)} %max.11, pred[8,8]{0,1:T(8,128)(4,1)S(1)} %copy.144, ...), kind=kOutput, calls=%fused_computation.41.clone.1 | convolution fusion | flops 275775488 | bytes 12910660 | tf_op jit(solution)/shard_map/while/body/nqhk,hkd->nqhd/dot_general | solution.py:147
  217.2 52.2 %all_to_all.61 = bf16[8,128,1024]{1,2,0:T(8,128)(2,1)S(1)} all-to-all(bf16[8,128,1024]{1,2,0:T(8,128)(2,1)S(1)} %bitcast.135), channel_id=1, replica_groups=mesh['grp'=4,'uly'=8] {'uly'}, dimensions={0} | all-to-all | bytes 4194304 | tf_op jit(solution)/shard_map/all_to_all | solution.py:156
  (186 shorter events, 90.7 us)
Async XLA Ops:
  6.5 22.6 %copy-start.4 = (bf16[128,8192]{1,0:T(8,128)(2,1)S(1)}, bf16[128,8192]{1,0:T(8,128)(2,1)}, u32[]{:S(2)}) copy-start(bf16[128,8192]{1,0:T(8,128)(2,1)} %param.12) | copy-start | bytes 6291460
  9.3 16.2 %all-to-all-start = ((bf16[128,8,128]{2,0,1:T(8,128)(2,1)}), bf16[128,8,128]{2,0,1:T(8,128)(2,1)S(1)}, u32[]{:S(2)}, u32[]{:S(2)}) async-start(bf16[128,8,128]{2,0,1:T(8,128)(2,1)} %bitcast.1), calls=%async_computation | async-start | bytes 524288 | tf_op jit(solution)/shard_map/all_to_all | solution.py:50
  25.5 12.2 %all-to-all-start.2 = ((bf16[128,8,128]{2,0,1:T(8,128)(2,1)}), bf16[128,8,128]{2,0,1:T(8,128)(2,1)S(1)}, u32[]{:S(2)}, u32[]{:S(2)}) async-start(bf16[128,8,128]{2,0,1:T(8,128)(2,1)} %bitcast.10), calls=%async_computation.2 | async-start | bytes 524288 | tf_op jit(solution)/shard_map/all_to_all | solution.py:51
  29.1 12.2 %copy-start.6 = (s32[64,3]{0,1:T(4,128)S(1)}, s32[64,3]{0,1:T(4,128)}, u32[]{:S(2)}) copy-start(s32[64,3]{0,1:T(4,128)} %param.16) | copy-start | bytes 2308
  29.1 13.2 %copy-start.5 = (s32[64,6]{0,1:T(8,128)S(1)}, s32[64,6]{0,1:T(8,128)}, u32[]{:S(2)}) copy-start(s32[64,6]{0,1:T(8,128)} %param.15) | copy-start | bytes 4612
  37.7 51.4 %all-to-all-start.1 = ((bf16[128,8,1024]{0,2,1:T(8,128)(2,1)}), bf16[128,8,1024]{0,2,1:T(8,128)(2,1)S(1)}, u32[]{:S(2)}, u32[]{:S(2)}) async-start(bf16[128,8,1024]{0,2,1:T(8,128)(2,1)} %bitcast.136), calls=%async_computation.1 | async-start | bytes 4194304 | tf_op jit(solution)/shard_map/all_to_all | solution.py:49
  41.3 112.6 %all-reduce.4.cloned.1.call-start = ((), (), s32[]{:S(2)}) async-start(), calls=%async_computation.4 | async-start | bytes 6291456 | tf_op jit(solution)/shard_map/psum | solution.py:76
  48.9 15.1 %collective-permute-start = (bf16[4,128,128]{2,1,0:T(8,128)(2,1)S(1)}, bf16[4,128,128]{2,1,0:T(8,128)(2,1)S(1)}, u32[]{:S(2)}, u32[]{:S(2)}) collective-permute-start(bf16[4,128,128]{2,1,0:T(8,128)(2,1)S(1)} %slice.26), channel_id=1, source_target_pairs={{0,8},{8,16},{16,24},{1,9},{9,17},{17,25},{2,10},{10,18},{18,26},{... | collective-permute-start | bytes 393224 | tf_op jit(solution)/shard_map/ppermute | solution.py:19
  50.2 13.9 %collective-permute-start.1 = (bf16[4,128,128]{2,1,0:T(8,128)(2,1)S(1)}, bf16[4,128,128]{2,1,0:T(8,128)(2,1)}, u32[]{:S(2)}, u32[]{:S(2)}) collective-permute-start(bf16[4,128,128]{2,1,0:T(8,128)(2,1)S(1)} %slice.27), channel_id=1, source_target_pairs={{0,8},{8,16},{16,24},{1,9},{9,17},{17,25},{2,10},{10,18},{18,26},{... | collective-permute-start | bytes 393224 | tf_op jit(solution)/shard_map/ppermute | solution.py:19
  89.1 3.4 %copy-start.3 = (bf16[128,8,1024]{0,2,1:T(8,128)(2,1)}, bf16[128,8,1024]{0,2,1:T(8,128)(2,1)S(1)}, u32[]{:S(2)}) copy-start(bf16[128,8,1024]{0,2,1:T(8,128)(2,1)S(1)} %all-to-all-done.1) | copy-start | bytes 6291460
  102.0 1.9 copy-start
  118.3 1.9 copy-start
  134.4 1.9 copy-start
  154.8 3.9 %copy-start.1 = (f32[8,128,8,128]{1,3,0,2:T(8,128)S(1)}, f32[8,128,8,128]{1,3,0,2:T(8,128)}, u32[]{:S(2)}) copy-start(f32[8,128,8,128]{1,3,0,2:T(8,128)} %get-tuple-element.534) | copy-start | bytes 12582916 | tf_op jit(solution)/shard_map/while
  161.9 1.9 copy-start.2
  164.8 3.9 %copy-start.1 = (f32[8,128,8,128]{1,3,0,2:T(8,128)S(1)}, f32[8,128,8,128]{1,3,0,2:T(8,128)}, u32[]{:S(2)}) copy-start(f32[8,128,8,128]{1,3,0,2:T(8,128)} %get-tuple-element.534) | copy-start | bytes 12582916 | tf_op jit(solution)/shard_map/while
  171.9 1.9 copy-start.2
  174.8 3.9 %copy-start.1 = (f32[8,128,8,128]{1,3,0,2:T(8,128)S(1)}, f32[8,128,8,128]{1,3,0,2:T(8,128)}, u32[]{:S(2)}) copy-start(f32[8,128,8,128]{1,3,0,2:T(8,128)} %get-tuple-element.534) | copy-start | bytes 12582916 | tf_op jit(solution)/shard_map/while
  181.9 1.9 copy-start.2
  184.8 3.9 %copy-start.1 = (f32[8,128,8,128]{1,3,0,2:T(8,128)S(1)}, f32[8,128,8,128]{1,3,0,2:T(8,128)}, u32[]{:S(2)}) copy-start(f32[8,128,8,128]{1,3,0,2:T(8,128)} %get-tuple-element.534) | copy-start | bytes 12582916 | tf_op jit(solution)/shard_map/while
  191.8 1.9 copy-start.2
  194.8 3.9 %copy-start.1 = (f32[8,128,8,128]{1,3,0,2:T(8,128)S(1)}, f32[8,128,8,128]{1,3,0,2:T(8,128)}, u32[]{:S(2)}) copy-start(f32[8,128,8,128]{1,3,0,2:T(8,128)} %get-tuple-element.534) | copy-start | bytes 12582916 | tf_op jit(solution)/shard_map/while
  201.8 1.9 copy-start.2
  204.7 3.9 %copy-start.1 = (f32[8,128,8,128]{1,3,0,2:T(8,128)S(1)}, f32[8,128,8,128]{1,3,0,2:T(8,128)}, u32[]{:S(2)}) copy-start(f32[8,128,8,128]{1,3,0,2:T(8,128)} %get-tuple-element.534) | copy-start | bytes 12582916 | tf_op jit(solution)/shard_map/while
  (1 other events, 1.9 us)
Sparse Core Ops, SparseCore 0:
  64.1 68.8 all-reduce.3
where the time goes:
time: 280 us; the launch traced here: 279 us
  matrix products  66.8 us (24%)
  local copies, waits for them, and re-layouts  55.3 us (20%)
  blocking collectives  52.2 us (19%)
  waiting for transfers between devices  36.5 us (13%)
  other arithmetic  25.7 us (9%)
  starting transfers between devices  20.6 us (7%)
  between operations  13.6 us (5%)
  loops' own time  8.45 us (3%)
    all_to_all x1, blocking collectives, shards(): lax.all_to_all(mixed, 'uly', split_axis=0, concat_axis=1, tiled=True)  52.2 us
    all_to_all x1, waiting for transfers between devices, shards(): lax.all_to_all(queries, 'uly', split_axis=1, concat_axis=0, tiled=True)  24.1 us
    dot_general x3, matrix products, weigh_near(): jnp.einsum('nqhk,hnkd->nqhd', prob_low, v_near, preferred_element_type=jn...  21.5 us
    dot_general x6, matrix products, weigh_far(): jnp.einsum('nqhk,hkd->nqhd', prob_low, v_far, preferred_element_type=jnp....  19 us
    while x39, local copies, waits for them, and re-layouts  17.3 us
    unnamed x20, local copies, waits for them, and re-layouts  15.5 us
    reduce_sum x9, other arithmetic, add_slot(): total = total * factor + jnp.sum(weights, axis=-1)  13.3 us
    dot_general x6, matrix products, vert_slot(): jnp.einsum('nqhd,hkd->nqhk', q_tiles, k_far, preferred_element_type=jnp.f...  12.9 us
  transfers between devices with their start and end apart: 6, of which 3 were waited for; matrix products, arithmetic and copies ran while one was open for 28% of the time, Pallas kernels for 0%

commit v1 on v0

--- a/solution.py
+++ b/solution.py
@@ -1,7 +1,11 @@
+import functools
+
 import jax
 import jax.numpy as jnp
 import numpy as np
 from jax import lax
+from jax.experimental import pallas as pl
+from jax.experimental.pallas import tpu as pltpu
 from jax.sharding import PartitionSpec as P
 
 QUERY_HEADS = 64
@@ -157,9 +161,294 @@
     return returned
 
 
+MESH = pl.DeviceIdType.MESH
+GATHERED_BYTES_MAX = 1 << 25
+LOG2_E = 1.4426950408889634
+
+
+def block_places(group_count, uly_count):
+    x_count, z_count = group_count // 2, uly_count // 2
+    block = np.arange(group_count * uly_count)
+    group, member = block // uly_count, block % uly_count
+    x, core, z, y = group // 2, group % 2, member // 2, member % 2
+    key_place = ((core * x_count + x) * 2 + y) * z_count + z
+    value_place = ((core * 2 + y) * x_count + x) * z_count + z
+    return key_place.astype(np.int32), value_place.astype(np.int32)
+
+
+def gather_kernel(
+    group_count, uly_count, k_ref, v_ref, k_out, v_out, own_sem, send_sem, recv_sem
+):
+    x_count, z_count = group_count // 2, uly_count // 2
+    group, member = lax.axis_index("grp"), lax.axis_index("uly")
+    x, core = group // 2, group % 2
+    z, y = member // 2, member % 2
+    heads = k_out.shape[0]
+
+    z_peers = [(group, lax.rem(z + d, z_count) * 2 + y) for d in range(1, z_count)]
+    y_peers = [(group, z * 2 + 1 - y)]
+    x_peers = [(lax.rem(x + d, x_count) * 2 + core, member) for d in range(1, x_count)]
+    core_peers = [(x * 2 + 1 - core, member)]
+    first_x = z_count - 1
+    first_y = first_x + x_count - 1
+    first_core = first_y + 1
+
+    barrier = pltpu.get_barrier_semaphore()
+    everyone = z_peers + y_peers + x_peers + core_peers
+    for peer in everyone:
+        pl.semaphore_signal(barrier, inc=1, device_id=peer, device_id_type=MESH)
+    pl.semaphore_wait(barrier, len(everyone))
+
+    def remote(source, target, item, number, peer):
+        return pltpu.make_async_remote_copy(
+            src_ref=source,
+            dst_ref=target,
+            send_sem=send_sem.at[item, number],
+            recv_sem=recv_sem.at[item, number],
+            device_id=peer,
+            device_id_type=MESH,
+        )
+
+    k_own = ((core * x_count + x) * 2 + y) * z_count + z
+    v_own = ((core * 2 + y) * x_count + x) * z_count + z
+    all_copies = []
+
+    def slab_copies(out, head, item, start, count, first, peers):
+        slab = out.at[head, pl.ds(start, count)]
+        return [remote(slab, slab, item, first + n, peer) for n, peer in enumerate(peers)]
+
+    own, along_z = [], []
+    for head in range(heads):
+        for item, source, out, place in (
+            (2 * head, k_ref, k_out, k_own),
+            (2 * head + 1, v_ref, v_out, v_own),
+        ):
+            columns = source.at[:, pl.ds(head * HEAD_SIZE, HEAD_SIZE)]
+            slot = out.at[head, place]
+            local = pltpu.make_async_copy(columns, slot, own_sem.at[item])
+            sends = [remote(columns, slot, item, n, peer) for n, peer in enumerate(z_peers)]
+            for copy in sends:
+                copy.start()
+            local.start()
+            own.append(local)
+            along_z.append(sends)
+            all_copies += sends
+
+    second, third, fourth = {}, {}, {}
+
+    def started(copies):
+        for copy in copies:
+            copy.start()
+        all_copies.extend(copies)
+        return copies
+
+    def arrived(copies):
+        for copy in copies:
+            copy.wait_recv()
+
+    for step in range(heads + 3):
+        head = step
+        if head < heads:
+            k_item, v_item = 2 * head, 2 * head + 1
+            own[k_item].wait()
+            arrived(along_z[k_item])
+            second[k_item] = started(
+                slab_copies(k_out, head, k_item, k_own - z, z_count, first_y, y_peers)
+            )
+            own[v_item].wait()
+            arrived(along_z[v_item])
+            second[v_item] = started(
+                slab_copies(v_out, head, v_item, v_own - z, z_count, first_x, x_peers)
+            )
+        head = step - 1
+        if 0 <= head < heads:
+            k_item, v_item = 2 * head, 2 * head + 1
+            arrived(second[k_item])
+            start = (core * x_count + x) * 2 * z_count
+            third[k_item] = started(
+                slab_copies(k_out, head, k_item, start, 2 * z_count, first_x, x_peers)
+            )
+            arrived(second[v_item])
+            start = (core * 2 + y) * x_count * z_count
+            third[v_item] = started(
+                slab_copies(v_out, head, v_item, start, x_count * z_count, first_y, y_peers)
+            )
+        head = step - 2
+        if 0 <= head < heads:
+            half = 2 * x_count * z_count
+            for item, out in ((2 * head, k_out), (2 * head + 1, v_out)):
+                arrived(third[item])
+                fourth[item] = started(
+                    slab_copies(out, head, item, core * half, half, first_core, core_peers)
+                )
+        head = step - 3
+        if 0 <= head < heads:
+            arrived(fourth[2 * head])
+            arrived(fourth[2 * head + 1])
+    for copy in all_copies:
+        copy.wait_send()
+
+
+def gathered(key_rows, value_rows, group_count, uly_count):
+    blocks = group_count * uly_count
+    shape = jax.ShapeDtypeStruct(
+        (KEY_VALUE_HEADS, blocks, BLOCK_TOKENS, HEAD_SIZE), key_rows.dtype
+    )
+    copies = uly_count // 2 - 1 + group_count // 2 - 1 + 2
+    items = 2 * KEY_VALUE_HEADS
+    return pl.pallas_call(
+        functools.partial(gather_kernel, group_count, uly_count),
+        out_shape=(shape, shape),
+        in_specs=[pl.BlockSpec(memory_space=pltpu.VMEM)] * 2,
+        out_specs=(pl.BlockSpec(memory_space=pl.ANY),) * 2,
+        scratch_shapes=[
+            pltpu.SemaphoreType.DMA((items,)),
+            pltpu.SemaphoreType.DMA((items, copies)),
+            pltpu.SemaphoreType.DMA((items, copies)),
+        ],
+        compiler_params=pltpu.CompilerParams(collective_id=0, has_side_effects=True),
+        name="gather_blocks",
+    )(key_rows, value_rows)
+
+
+def attend_kernel(
+    variants,
+    here_ref,
+    key_place,
+    value_place,
+    vert_ref,
+    slash_ref,
+    q_ref,
+    k_ref,
+    v_ref,
+    out_ref,
+    held,
+    counts,
+):
+    kv_head = pl.program_id(0)
+    per_group = q_ref.shape[1] // HEAD_SIZE
+    slash_slots, vert_slots = slash_ref.shape[1], vert_ref.shape[1]
+    here = here_ref[0]
+
+    @pl.loop(0, per_group)
+    def _(local):
+        head = kv_head * per_group + local
+        for slot in range(slash_slots + vert_slots):
+            held[local, slot] = here
+        filled = jnp.int32(0)
+        offsets = [slash_ref[head, slot] for slot in range(slash_slots)]
+        for offset in offsets:
+            held[local, filled] = here - offset
+            ok = (offset >= 1) & (here - offset >= 0)
+            filled = filled + ok.astype(jnp.int32)
+        for slot in range(vert_slots):
+            block = vert_ref[head, slot]
+            ok = (block >= 0) & (block < here)
+            for offset in offsets:
+                ok = ok & jnp.logical_not((offset >= 1) & (here - offset == block))
+            held[local, filled] = block
+            filled = filled + ok.astype(jnp.int32)
+        counts[local] = filled
+
+    rate = HEAD_SIZE ** (-0.5) * LOG2_E
+    causal = lax.broadcasted_iota(
+        jnp.int32, (BLOCK_TOKENS, BLOCK_TOKENS), 0
+    ) >= lax.broadcasted_iota(jnp.int32, (BLOCK_TOKENS, BLOCK_TOKENS), 1)
+
+    def attend(local, extra):
+        columns = pl.ds(pl.multiple_of(local * HEAD_SIZE, HEAD_SIZE), HEAD_SIZE)
+        q = q_ref[:, columns]
+        filled = counts[local]
+        blocks = [here]
+        for slot in range(extra):
+            blocks.append(jnp.where(slot < filled, held[local, slot], here))
+        keys = jnp.concatenate([k_ref[0, key_place[block]] for block in blocks], axis=0)
+        values = jnp.concatenate([v_ref[0, value_place[block]] for block in blocks], axis=0)
+        scores = lax.dot_general(
+            q, keys, (((1,), (1,)), ((), ())), preferred_element_type=jnp.float32
+        )
+        pieces = [
+            scores[:, n * BLOCK_TOKENS : (n + 1) * BLOCK_TOKENS] for n in range(extra + 1)
+        ]
+        pieces[0] = jnp.where(causal, pieces[0], neg_large)
+        for slot in range(extra):
+            bias = jnp.where(slot < filled, 0.0, neg_large).astype(jnp.float32)
+            pieces[slot + 1] = pieces[slot + 1] + bias
+        best = pieces[0]
+        for piece in pieces[1:]:
+            best = jnp.maximum(best, piece)
+        best = jnp.max(best, axis=1, keepdims=True)
+        weights = [jnp.exp2((piece - best) * rate) for piece in pieces]
+        total = weights[0]
+        for weight in weights[1:]:
+            total = total + weight
+        total = jnp.sum(total, axis=1, keepdims=True)
+        probs = jnp.concatenate([weight.astype(jnp.bfloat16) for weight in weights], axis=1)
+        mixed = jnp.dot(probs, values, preferred_element_type=jnp.float32)
+        out_ref[:, columns] = (mixed / total).astype(out_ref.dtype)
+
+    @pl.loop(0, per_group // 2)
+    def _(pair):
+        one, two = 2 * pair, 2 * pair + 1
+        most = jnp.maximum(counts[one], counts[two])
+        below = -1
+        for extra in variants:
+
+            @pl.when((most > below) & (most <= extra))
+            def _(extra=extra):
+                attend(one, extra)
+                attend(two, extra)
+
+            below = extra
+
+
+def attended_here(queries, keys, values, vert_blocks, slash_offsets, here, places):
+    tokens, width = queries.shape
+    blocks = keys.shape[1]
+    per_group = QUERY_HEADS // KEY_VALUE_HEADS
+    slots = vert_blocks.shape[1] + slash_offsets.shape[1]
+    variants = sorted({min(n, slots) for n in range(1, slots + 2, 2)})
+    wide = pl.BlockSpec((tokens, per_group * HEAD_SIZE), lambda n, *_: (0, n))
+    held = pl.BlockSpec((1, blocks, BLOCK_TOKENS, HEAD_SIZE), lambda n, *_: (n, 0, 0, 0))
+    return pl.pallas_call(
+        functools.partial(attend_kernel, variants),
+        out_shape=jax.ShapeDtypeStruct((tokens, width), queries.dtype),
+        grid_spec=pltpu.PrefetchScalarGridSpec(
+            num_scalar_prefetch=5,
+            grid=(KEY_VALUE_HEADS,),
+            in_specs=[wide, held, held],
+            out_specs=wide,
+            scratch_shapes=[
+                pltpu.SMEM((per_group, slots + 1), jnp.int32),
+                pltpu.SMEM((per_group,), jnp.int32),
+            ],
+        ),
+        compiler_params=pltpu.CompilerParams(dimension_semantics=("arbitrary",)),
+        name="attend_blocks",
+    )(here, *places, vert_blocks, slash_offsets, queries, keys, values)
+
+
+def resident_shards(queries, key_state_rows, value_state_rows, vert_blocks, slash_offsets):
+    group_count, uly_count = lax.axis_size("grp"), lax.axis_size("uly")
+    here = (lax.axis_index("grp") * uly_count + lax.axis_index("uly")).astype(jnp.int32)
+    keys, values = gathered(key_state_rows, value_state_rows, group_count, uly_count)
+    places = [jnp.asarray(place) for place in block_places(group_count, uly_count)]
+    return attended_here(
+        queries, keys, values, vert_blocks, slash_offsets, here.reshape(1), places
+    )
+
+
+def chosen(queries, key_state_rows, *rest):
+    devices = lax.axis_size("grp") * lax.axis_size("uly")
+    gathered_bytes = 2 * devices * key_state_rows.size * key_state_rows.dtype.itemsize
+    fits = gathered_bytes <= GATHERED_BYTES_MAX and queries.shape[0] == BLOCK_TOKENS
+    plan = resident_shards if fits else shards
+    return plan(queries, key_state_rows, *rest)
+
+
 def solution(mesh):
     return jax.shard_map(
-        shards,
+        chosen,
         mesh=mesh,
         in_specs=(
             P(("grp", "uly"), None),

time: 280 us -> 130 us (0.46)
  the two profiles are of different devices: /device:TPU:0 before, /device:TPU:15 now
where the time goes in v1:
time: 130 us
  Pallas kernels  127 us (98%)
  local copies, waits for them, and re-layouts  2.77 us (2%)
    pallas_call x1, Pallas kernels, gathered(): pl.pallas_call(functools.partial(gather_kernel, group_count, uly_count),...  91.2 us
    pallas_call x1, Pallas kernels, attended_here(): pl.pallas_call(functools.partial(attend_kernel, variants), out_shape=jax....  35.9 us
    unnamed x2, local copies, waits for them, and re-layouts  2.77 us

profile of v1, /device:TPU:15, one launch (start us, length us, event | category | flops | bytes accessed | tf_op | source)
XLA Modules:
  0.0 129.9 jit_solution(3738612503608219165)
XLA Ops:
  0.0 1.4 %copy.8.vert_ref = s32[64,6]{1,0:T(8,128)} copy(s32[64,6]{0,1:T(8,128)} %param.10) | data formatting | bytes 3072 | tf_op args[3]
  1.4 1.4 %copy.9.slash_ref = s32[64,3]{1,0:T(8,128)} copy(s32[64,3]{0,1:T(4,128)} %param.11) | data formatting | bytes 1536 | tf_op args[4]
  2.8 91.2 %gather_blocks.1 = (bf16[8,32,128,128]{3,2,1,0:T(8,128)(2,1)}, bf16[8,32,128,128]{3,2,1,0:T(8,128)(2,1)}) custom-call(bf16[128,1024]{1,0:T(8,128)(2,1)} %k_ref.1, bf16[128,1024]{1,0:T(8,128)(2,1)} %v_ref.1), custom_call_target="tpu_custom_call" | custom-call | tf_op jit(solution)/shard_map/gather_blocks/pallas_call | solution.py:299
  94.0 35.9 %attend_blocks.1 = bf16[128,8192]{1,0:T(8,128)(2,1)} custom-call(s32[1]{0:T(128)} %bitcast.here_ref, s32[32]{0:T(128)} %constant.14.clone.key_place, s32[32]{0:T(128)} %constant.15.clone.value_place, s32[64,6]{1,0:T(8,128)} %copy.8.vert_ref, s32[64,3]{1,0:T(8,128)} %copy.9.slash_ref, bf16[128,8192]{1,0:T(8,128)(2,1)} %q_ref.1, ...), custom_call_target="tpu_custom_call" | custom-call | tf_op jit(solution)/shard_map/attend_blocks/pallas_call | solution.py:413

commit v2 on v0

--- a/solution.py
+++ b/solution.py
@@ -1,7 +1,11 @@
+import functools
+
 import jax
 import jax.numpy as jnp
 import numpy as np
 from jax import lax
+from jax.experimental import pallas as pl
+from jax.experimental.pallas import tpu as pltpu
 from jax.sharding import PartitionSpec as P
 
 QUERY_HEADS = 64
@@ -157,9 +161,262 @@
     return returned
 
 
+MESH = pl.DeviceIdType.MESH
+GATHERED_BYTES_MAX = 1 << 25
+LOG2_E = 1.4426950408889634
+EARLY = ("zyx", "zxy")
+LATE = ("yzx", "xzy")
+
+
+def orders_of(head):
+    return LATE if head % 3 == 0 else EARLY
+
+
+def place_in(order, sizes, where):
+    place = where["core"]
+    for axis in reversed(order):
+        place = place * sizes[axis] + where[axis]
+    return place
+
+
+def sizes_of(group_count, uly_count):
+    return {"x": group_count // 2, "core": 2, "y": 2, "z": uly_count // 2}
+
+
+def whereabouts(group, member):
+    return {"x": group // 2, "core": group % 2, "y": member % 2, "z": member // 2}
+
+
+def place_table(group_count, uly_count):
+    block = np.arange(group_count * uly_count)
+    where = whereabouts(block // uly_count, block % uly_count)
+    sizes = sizes_of(group_count, uly_count)
+    rows = [place_in(order, sizes, where) for order in EARLY + LATE]
+    return np.stack(rows).astype(np.int32)
+
+
+def attend_all(orders, q_ref, k_buf, v_buf, place_ref, vert_ref, slash_ref, out_ref, head, here):
+    per_group = q_ref.shape[1] // (HEAD_SIZE * KEY_VALUE_HEADS)
+    slash_slots, vert_slots = slash_ref.shape[0], vert_ref.shape[0]
+    rate = HEAD_SIZE ** (-0.5) * LOG2_E
+    causal = lax.broadcasted_iota(
+        jnp.int32, (BLOCK_TOKENS, BLOCK_TOKENS), 0
+    ) >= lax.broadcasted_iota(jnp.int32, (BLOCK_TOKENS, BLOCK_TOKENS), 1)
+    k_row, v_row = ((EARLY + LATE).index(order) for order in orders)
+
+    def slots_of(q_head):
+        blocks, allowed = [here], [None]
+        offsets = [slash_ref[slot, q_head] for slot in range(slash_slots)]
+        for offset in offsets:
+            ok = (offset >= 1) & (here - offset >= 0)
+            blocks.append(jnp.where(ok, here - offset, here))
+            allowed.append(ok)
+        for slot in range(vert_slots):
+            block = vert_ref[slot, q_head]
+            ok = (block >= 0) & (block < here)
+            for offset in offsets:
+                ok = ok & jnp.logical_not((offset >= 1) & (here - offset == block))
+            blocks.append(jnp.where(ok, block, here))
+            allowed.append(ok)
+        return blocks, allowed
+
+    @pl.loop(0, per_group // GANG)
+    def _(turn):
+        chosen_slots, columns, scores = [], [], []
+        for n in range(GANG):
+            q_head = head * per_group + GANG * turn + n
+            columns.append(pl.ds(pl.multiple_of(q_head * HEAD_SIZE, HEAD_SIZE), HEAD_SIZE))
+            chosen_slots.append(slots_of(q_head))
+        for n in range(GANG):
+            blocks, _ = chosen_slots[n]
+            keys = jnp.concatenate([k_buf[place_ref[k_row, block]] for block in blocks], axis=0)
+            scores.append(
+                lax.dot_general(
+                    q_ref[:, columns[n]],
+                    keys,
+                    (((1,), (1,)), ((), ())),
+                    preferred_element_type=jnp.float32,
+                )
+            )
+        probs, totals = [], []
+        for n in range(GANG):
+            _, allowed = chosen_slots[n]
+            pieces = []
+            for slot, ok in enumerate(allowed):
+                piece = scores[n][:, slot * BLOCK_TOKENS : (slot + 1) * BLOCK_TOKENS]
+                if ok is None:
+                    pieces.append(jnp.where(causal, piece, neg_large))
+                else:
+                    pieces.append(piece + jnp.where(ok, 0.0, neg_large).astype(jnp.float32))
+            best = functools.reduce(jnp.maximum, pieces)
+            best = jnp.max(best, axis=1, keepdims=True)
+            weights = [jnp.exp2((piece - best) * rate) for piece in pieces]
+            total = functools.reduce(jnp.add, weights)
+            totals.append(jnp.sum(total, axis=1, keepdims=True))
+            probs.append(
+                jnp.concatenate([weight.astype(jnp.bfloat16) for weight in weights], axis=1)
+            )
+        for n in range(GANG):
+            blocks, _ = chosen_slots[n]
+            values = jnp.concatenate([v_buf[place_ref[v_row, block]] for block in blocks], axis=0)
+            mixed = jnp.dot(probs[n], values, preferred_element_type=jnp.float32)
+            out_ref[:, columns[n]] = (mixed / totals[n]).astype(out_ref.dtype)
+
+
+GANG = 2
+
+
+def resident_kernel(
+    group_count,
+    uly_count,
+    place_ref,
+    vert_ref,
+    slash_ref,
+    q_ref,
+    k_ref,
+    v_ref,
+    out_ref,
+    own_sem,
+    send_sem,
+    recv_sem,
+    *held,
+):
+    sizes = sizes_of(group_count, uly_count)
+    group, member = lax.axis_index("grp"), lax.axis_index("uly")
+    me = whereabouts(group, member)
+    here = group * uly_count + member
+    heads = KEY_VALUE_HEADS
+
+    def device_at(where):
+        return (where["x"] * 2 + where["core"], where["z"] * 2 + where["y"])
+
+    peers, first, used = {}, {}, 0
+    for axis in ("x", "y", "z", "core"):
+        count = sizes[axis]
+        peers[axis] = [
+            device_at({**me, axis: lax.rem(me[axis] + d, count)}) for d in range(1, count)
+        ]
+        first[axis] = used
+        used += count - 1
+
+    barrier = pltpu.get_barrier_semaphore()
+    everyone = [peer for group_peers in peers.values() for peer in group_peers]
+    for peer in everyone:
+        pl.semaphore_signal(barrier, inc=1, device_id=peer, device_id_type=MESH)
+    pl.semaphore_wait(barrier, len(everyone))
+
+    all_copies = []
+
+    def sent(source, target, item, axis):
+        copies = []
+        for n, peer in enumerate(peers[axis]):
+            copy = pltpu.make_async_remote_copy(
+                src_ref=source,
+                dst_ref=target,
+                send_sem=send_sem.at[item, first[axis] + n],
+                recv_sem=recv_sem.at[item, first[axis] + n],
+                device_id=peer,
+                device_id_type=MESH,
+            )
+            copy.start()
+            copies.append(copy)
+        all_copies.extend(copies)
+        return copies
+
+    flights, own = {}, {}
+    for head in range(heads):
+        for kind, source in enumerate((k_ref, v_ref)):
+            item, order = 2 * head + kind, orders_of(head)[kind]
+            slot = held[item].at[place_in(order, sizes, me)]
+            columns = source.at[:, pl.ds(head * HEAD_SIZE, HEAD_SIZE)]
+            flights[item] = sent(columns, slot, item, order[0])
+            own[item] = pltpu.make_async_copy(columns, slot, own_sem.at[item])
+            own[item].start()
+
+    def forward(head, stage):
+        for kind in range(2):
+            item, order = 2 * head + kind, orders_of(head)[kind]
+            if stage == 1:
+                own[item].wait()
+            for copy in flights[item]:
+                copy.wait_recv()
+            if stage <= 3:
+                route = [*order, "core"]
+                start = {**me, **{axis: 0 for axis in route[:stage]}}
+                count = 1
+                for axis in route[:stage]:
+                    count *= sizes[axis]
+                slab = held[item].at[pl.ds(place_in(order, sizes, start), count)]
+                flights[item] = sent(slab, slab, item, route[stage])
+
+    for step in range(heads + 3):
+        if step < heads:
+            forward(step, 1)
+        if 0 <= step - 1 < heads:
+            forward(step - 1, 2)
+        if 0 <= step - 3 < heads:
+            head = step - 3
+            forward(head, 4)
+            attend_all(
+                orders_of(head),
+                q_ref,
+                held[2 * head],
+                held[2 * head + 1],
+                place_ref,
+                vert_ref,
+                slash_ref,
+                out_ref,
+                head,
+                here,
+            )
+        if 0 <= step - 2 < heads:
+            forward(step - 2, 3)
+    for copy in all_copies:
+        copy.wait_send()
+
+
+def resident_shards(queries, key_state_rows, value_state_rows, vert_blocks, slash_offsets):
+    group_count, uly_count = lax.axis_size("grp"), lax.axis_size("uly")
+    sizes = sizes_of(group_count, uly_count)
+    copies = sum(count - 1 for count in sizes.values())
+    items = 2 * KEY_VALUE_HEADS
+    blocks = group_count * uly_count
+    vmem = pl.BlockSpec(memory_space=pltpu.VMEM)
+    smem = pl.BlockSpec(memory_space=pltpu.SMEM)
+    return pl.pallas_call(
+        functools.partial(resident_kernel, group_count, uly_count),
+        out_shape=jax.ShapeDtypeStruct(queries.shape, queries.dtype),
+        in_specs=[smem, smem, smem, vmem, vmem, vmem],
+        out_specs=vmem,
+        scratch_shapes=[
+            pltpu.SemaphoreType.DMA((items,)),
+            pltpu.SemaphoreType.DMA((items, copies)),
+            pltpu.SemaphoreType.DMA((items, copies)),
+        ]
+        + [pltpu.VMEM((blocks, BLOCK_TOKENS, HEAD_SIZE), key_state_rows.dtype)] * items,
+        compiler_params=pltpu.CompilerParams(collective_id=0, has_side_effects=True),
+        name="gather_and_attend",
+    )(
+        jnp.asarray(place_table(group_count, uly_count)),
+        vert_blocks.T,
+        slash_offsets.T,
+        queries,
+        key_state_rows,
+        value_state_rows,
+    )
+
+
+def chosen(queries, key_state_rows, *rest):
+    devices = lax.axis_size("grp") * lax.axis_size("uly")
+    gathered_bytes = 2 * devices * key_state_rows.size * key_state_rows.dtype.itemsize
+    fits = gathered_bytes <= GATHERED_BYTES_MAX and queries.shape[0] == BLOCK_TOKENS
+    plan = resident_shards if fits else shards
+    return plan(queries, key_state_rows, *rest)
+
+
 def solution(mesh):
     return jax.shard_map(
-        shards,
+        chosen,
         mesh=mesh,
         in_specs=(
             P(("grp", "uly"), None),

time: 280 us -> 117 us (0.42)
  Pallas kernels: 0 us -> 113 us
  matrix products: 66.8 us -> 0 us
  blocking collectives: 52.2 us -> 0 us
  local copies, waits for them, and re-layouts: 55.3 us -> 3.1 us
  waiting for transfers between devices: 36.5 us -> 0 us
  other arithmetic: 25.7 us -> 0 us
  starting transfers between devices: 20.6 us -> 0 us
  between operations: 13.6 us -> 0.01 us
  loops' own time: 8.45 us -> 0 us
    pallas_call x0 -> x1, Pallas kernels: none -> 113 us  [resident_shards(): pl.pallas_call(functools.partial(resident_kernel, group_count, uly_count)...]
    dot_general x20 -> x0, matrix products: 66.8 us -> none  [the longest x3 21.5 us: weigh_near(): jnp.einsum('nqhk,hnkd->nqhd', prob_low, v_near, preferred_element_type=jn...]
    all_to_all x1 -> x0, blocking collectives: 52.2 us -> none  [shards(): lax.all_to_all(mixed, 'uly', split_axis=0, concat_axis=1, tiled=True)]
    all_to_all x3 -> x0, waiting for transfers between devices: 36.5 us -> none  [the longest x1 24.1 us: shards(): lax.all_to_all(queries, 'uly', split_axis=1, concat_axis=0, tiled=True)]
    gather x14 -> x0, local copies, waits for them, and re-layouts: 18.5 us -> none  [the longest x2 4.57 us: shards(): key_block_tiles[local_block]]
    while x40 -> x0, local copies, waits for them, and re-layouts: 17.3 us -> none
    reduce_sum x12 -> x0, other arithmetic: 14.9 us -> none  [the longest x9 13.3 us: add_slot(): total = total * factor + jnp.sum(weights, axis=-1)]
    all_to_all x3 -> x0, starting transfers between devices: 14.5 us -> none  [the longest x1 7.31 us: shards(): lax.all_to_all(key_outgoing, 'uly', split_axis=1, concat_axis=0, tiled=True)]
  transfers between devices with their start and end apart: 6 -> 0, of which waited for: 3 -> 0; matrix products, arithmetic and copies ran while one was open for 28% -> 0% of each run, Pallas kernels for 0% -> 0%
where the time goes in v2:
time: 117 us
  Pallas kernels  113 us (97%)
  local copies, waits for them, and re-layouts  3.1 us (3%)
    pallas_call x1, Pallas kernels, resident_shards(): pl.pallas_call(functools.partial(resident_kernel, group_count, uly_count)...  113 us
    unnamed x1, local copies, waits for them, and re-layouts  3.1 us

profile of v2, /device:TPU:0, one launch (start us, length us, event | category | flops | bytes accessed | tf_op | source)
XLA Modules:
  0.0 116.5 jit_solution(8784848760903618058)
XLA Ops:
  0.0 113.4 %gather_and_attend.1 = bf16[128,8192]{1,0:T(8,128)(2,1)} custom-call(s32[4,32]{1,0:T(4,128)} %constant.2.clone.place_ref, s32[6,64]{1,0:T(8,128)} %bitcast.2, s32[3,64]{1,0:T(4,128)} %bitcast.3, bf16[128,8192]{1,0:T(8,128)(2,1)} %q_ref.1, bf16[128,1024]{1,0:T(8,128)(2,1)} %k_ref.1, bf16[128,1024]{1,0:T(8,128)(2,1)} %v_ref.1), custom_call_target="tpu_custom_call" | custom-call | tf_op jit(solution)/shard_map/gather_and_attend/pallas_call | solution.py:386
  113.4 3.1 %copy.8 = bf16[128,8192]{1,0:T(8,128)(2,1)} copy(bf16[128,8192]{1,0:T(8,128)(2,1)} %gather_and_attend.1) | data formatting | bytes 4194304

commit v3 on v2

--- a/solution.py
+++ b/solution.py
@@ -169,7 +169,7 @@
 
 
 def orders_of(head):
-    return LATE if head % 3 == 0 else EARLY
+    return LATE if head % 3 == 1 else EARLY
 
 
 def place_in(order, sizes, where):
@@ -263,7 +263,8 @@
             out_ref[:, columns[n]] = (mixed / totals[n]).astype(out_ref.dtype)
 
 
-GANG = 2
+GANG = 4
+AHEAD = 2
 
 
 def resident_kernel(
@@ -324,7 +325,8 @@
         return copies
 
     flights, own = {}, {}
-    for head in range(heads):
+
+    def begin(head):
         for kind, source in enumerate((k_ref, v_ref)):
             item, order = 2 * head + kind, orders_of(head)[kind]
             slot = held[item].at[place_in(order, sizes, me)]
@@ -332,6 +334,9 @@
             flights[item] = sent(columns, slot, item, order[0])
             own[item] = pltpu.make_async_copy(columns, slot, own_sem.at[item])
             own[item].start()
+
+    for head in range(min(AHEAD, heads)):
+        begin(head)
 
     def forward(head, stage):
         for kind in range(2):
@@ -350,6 +355,8 @@
                 flights[item] = sent(slab, slab, item, route[stage])
 
     for step in range(heads + 3):
+        if step + AHEAD < heads:
+            begin(step + AHEAD)
         if step < heads:
             forward(step, 1)
         if 0 <= step - 1 < heads:

time: 117 us -> 97.6 us (0.83)
  Pallas kernels: 113 us -> 94.3 us
    pallas_call x1, Pallas kernels: 113 us -> 94.3 us  [resident_shards(): pl.pallas_call(functools.partial(resident_kernel, group_count, uly_count)...]
where the time goes in v3:
time: 97.6 us; the launch traced here: 97.4 us
  Pallas kernels  94.3 us (97%)
  local copies, waits for them, and re-layouts  3.1 us (3%)
    pallas_call x1, Pallas kernels, resident_shards(): pl.pallas_call(functools.partial(resident_kernel, group_count, uly_count)...  94.3 us
    unnamed x1, local copies, waits for them, and re-layouts  3.1 us

profile of v3, /device:TPU:0, one launch (start us, length us, event | category | flops | bytes accessed | tf_op | source)
XLA Modules:
  0.0 97.4 jit_solution(17137332481727657342)
XLA Ops:
  0.0 94.3 %gather_and_attend.1 = bf16[128,8192]{1,0:T(8,128)(2,1)} custom-call(s32[4,32]{1,0:T(4,128)} %constant.2.clone.place_ref, s32[6,64]{1,0:T(8,128)} %bitcast.2, s32[3,64]{1,0:T(4,128)} %bitcast.3, bf16[128,8192]{1,0:T(8,128)(2,1)} %q_ref.1, bf16[128,1024]{1,0:T(8,128)(2,1)} %k_ref.1, bf16[128,1024]{1,0:T(8,128)(2,1)} %v_ref.1), custom_call_target="tpu_custom_call" | custom-call | tf_op jit(solution)/shard_map/gather_and_attend/pallas_call | solution.py:393
  94.3 3.1 %copy.8 = bf16[128,8192]{1,0:T(8,128)(2,1)} copy(bf16[128,8192]{1,0:T(8,128)(2,1)} %gather_and_attend.1) | data formatting | bytes 4194304

commit v4 on v3

--- a/solution.py
+++ b/solution.py
@@ -264,7 +264,7 @@
 
 
 GANG = 4
-AHEAD = 2
+AHEAD = 1
 
 
 def resident_kernel(
@@ -273,10 +273,14 @@
     place_ref,
     vert_ref,
     slash_ref,
-    q_ref,
+    q_hbm,
     k_ref,
     v_ref,
+    out_hbm,
+    q_ref,
     out_ref,
+    q_sem,
+    out_sem,
     own_sem,
     send_sem,
     recv_sem,
@@ -287,6 +291,10 @@
     me = whereabouts(group, member)
     here = group * uly_count + member
     heads = KEY_VALUE_HEADS
+    per_head = q_hbm.shape[1] // heads
+    q_copy = pltpu.make_async_copy(q_hbm, q_ref, q_sem)
+    q_copy.start()
+    out_copies = []
 
     def device_at(where):
         return (where["x"] * 2 + where["core"], where["z"] * 2 + where["y"])
@@ -334,9 +342,6 @@
             flights[item] = sent(columns, slot, item, order[0])
             own[item] = pltpu.make_async_copy(columns, slot, own_sem.at[item])
             own[item].start()
-
-    for head in range(min(AHEAD, heads)):
-        begin(head)
 
     def forward(head, stage):
         for kind in range(2):
@@ -354,16 +359,29 @@
                 slab = held[item].at[pl.ds(place_in(order, sizes, start), count)]
                 flights[item] = sent(slab, slab, item, route[stage])
 
+    def along_z(head):
+        if orders_of(head) == LATE:
+            forward(head, 1)
+        else:
+            begin(head)
+
+    for head in range(heads):
+        if orders_of(head) == LATE:
+            begin(head)
+    for head in range(min(AHEAD, heads)):
+        along_z(head)
     for step in range(heads + 3):
         if step + AHEAD < heads:
-            begin(step + AHEAD)
-        if step < heads:
+            along_z(step + AHEAD)
+        if step < heads and orders_of(step) == EARLY:
             forward(step, 1)
         if 0 <= step - 1 < heads:
             forward(step - 1, 2)
         if 0 <= step - 3 < heads:
             head = step - 3
             forward(head, 4)
+            if head == 0:
+                q_copy.wait()
             attend_all(
                 orders_of(head),
                 q_ref,
@@ -376,10 +394,19 @@
                 head,
                 here,
             )
+            columns = pl.ds(head * per_head, per_head)
+            out_copies.append(
+                pltpu.make_async_copy(
+                    out_ref.at[:, columns], out_hbm.at[:, columns], out_sem.at[head]
+                )
+            )
+            out_copies[-1].start()
         if 0 <= step - 2 < heads:
             forward(step - 2, 3)
     for copy in all_copies:
         copy.wait_send()
+    for copy in out_copies:
+        copy.wait()
 
 
 def resident_shards(queries, key_state_rows, value_state_rows, vert_blocks, slash_offsets):
@@ -390,12 +417,17 @@
     blocks = group_count * uly_count
     vmem = pl.BlockSpec(memory_space=pltpu.VMEM)
     smem = pl.BlockSpec(memory_space=pltpu.SMEM)
+    hbm = pl.BlockSpec(memory_space=pl.ANY)
     return pl.pallas_call(
         functools.partial(resident_kernel, group_count, uly_count),
         out_shape=jax.ShapeDtypeStruct(queries.shape, queries.dtype),
-        in_specs=[smem, smem, smem, vmem, vmem, vmem],
-        out_specs=vmem,
+        in_specs=[smem, smem, smem, hbm, vmem, vmem],
+        out_specs=hbm,
         scratch_shapes=[
+            pltpu.VMEM(queries.shape, queries.dtype),
+            pltpu.VMEM(queries.shape, queries.dtype),
+            pltpu.SemaphoreType.DMA,
+            pltpu.SemaphoreType.DMA((KEY_VALUE_HEADS,)),
             pltpu.SemaphoreType.DMA((items,)),
             pltpu.SemaphoreType.DMA((items, copies)),
             pltpu.SemaphoreType.DMA((items, copies)),

time: 97.6 us -> 96.2 us (0.986)
  Pallas kernels: 94.3 us -> 93 us
    pallas_call x1, Pallas kernels: 94.3 us -> 93 us  [resident_shards(): pl.pallas_call(functools.partial(resident_kernel, group_count, uly_count)...]
where the time goes in v4:
time: 96.2 us; the launch traced here: 96.1 us
  Pallas kernels  93 us (97%)
  local copies, waits for them, and re-layouts  3.1 us (3%)
    pallas_call x1, Pallas kernels, resident_shards(): pl.pallas_call(functools.partial(resident_kernel, group_count, uly_count)...  93 us
    unnamed x1, local copies, waits for them, and re-layouts  3.1 us

profile of v4, /device:TPU:0, one launch (start us, length us, event | category | flops | bytes accessed | tf_op | source)
XLA Modules:
  0.0 96.1 jit_solution(15843957523084097958)
XLA Ops:
  0.0 93.0 %gather_and_attend.1 = bf16[128,8192]{1,0:T(8,128)(2,1)} custom-call(s32[4,32]{1,0:T(4,128)} %constant.2.clone.place_ref, s32[6,64]{1,0:T(8,128)} %bitcast.2, s32[3,64]{1,0:T(4,128)} %bitcast.3, bf16[128,8192]{1,0:T(8,128)(2,1)} %q_hbm.1, bf16[128,1024]{1,0:T(8,128)(2,1)} %k_ref.1, bf16[128,1024]{1,0:T(8,128)(2,1)} %v_ref.1), custom_call_target="tpu_custom_call" | custom-call | tf_op jit(solution)/shard_map/gather_and_attend/pallas_call | solution.py:421
  93.0 3.1 %copy.8 = bf16[128,8192]{1,0:T(8,128)(2,1)} copy(bf16[128,8192]{1,0:T(8,128)(2,1)} %gather_and_attend.1) | data formatting | bytes 4194304
